TPU v7x, 32 devices: a whole 2x2x4 slice. The times are simulated.
32 devices in a mesh: chan: 8 (over z, y), win: 4 (over x, core).
Axes of the slice: x: 2, y: 2, z: 4, core: 2. Of those that a mesh axis runs over, the one named last changes fastest.
Arguments:
- samples: bfloat16 [8, 256, 6144], P('win', 'chan'), may hold values from -6 to 6
- pair_offsets: int32 [8, 3], P('chan'), may hold values from 0 to 2, each once within a row
- spectral_slot_position: int32 [1024], replicated, may hold values from 1 to 3071, as said below
Outputs:
- correlations: float32 [256, 3, 2, 32, 1024], P('chan', None, None, None, 'win')
Inputs may be any that keep to these rules, and one draw needn't show every extreme that they name: `pair_offsets`: each row holds every offset of 0 to 2 once. `spectral_slot_position`: distinct and rising; the first is 1 and the last is 3071.
All inputs are finite; a program needn't handle non-finite values.
Results may differ from a plain program's by a relative error of at most 0.0036.
Values sent between devices are 32-bit elements; how exact they have to be, the bound alone decides.
No kernel may reach another device: no remote copies, remote signals or barrier semaphores. Data moves between devices by JAX's collectives and lax.ppermute only.
A program may use at most 64 MiB of HBM per device.

v0:
```python
import math
import jax
import jax.numpy as jnp
from jax import lax
from jax.sharding import PartitionSpec as P

S = 6144
HALF = 64
TB = 1024
EPSILON = 1e-06


def passed_along(value, axis, steps):
    count = lax.axis_size(axis)
    leading, last = (max(0, -steps), min(count, count - steps))
    return lax.ppermute(value, axis, [(source, source + steps) for source in range(leading, last)])


def angle_parts(spectral_slot_position):
    factor = 2.0 * math.pi / S
    moments = jnp.arange(TB, dtype=jnp.int32)
    base = (moments[:, None] * spectral_slot_position[None, :] % S).astype(jnp.float32) * factor
    starts = jnp.arange(S // TB, dtype=jnp.int32) * TB
    turns = (starts[:, None] * spectral_slot_position[None, :] % S).astype(jnp.float32) * factor
    return (jnp.cos(base), jnp.sin(base), jnp.cos(turns), jnp.sin(turns))


def block_table(base_cos, base_sin, turn_cos, turn_sin):
    scale = 1.0 / math.sqrt(S)
    cos_part = (base_cos * turn_cos - base_sin * turn_sin) * scale
    sin_part = (base_sin * turn_cos + base_cos * turn_sin) * scale
    return jnp.concatenate([cos_part, sin_part], axis=-1).astype(jnp.bfloat16)


def whiten(spectra, half_width):
    freq_count = spectra.shape[-1]
    powers = spectra[..., 0, :] * spectra[..., 0, :] + spectra[..., 1, :] * spectra[..., 1, :]
    places = jnp.arange(freq_count, dtype=jnp.int32)
    banded = (jnp.abs(places[:, None] - places[None, :]) <= half_width).astype(jnp.float32)
    tallies = jnp.sum(banded, axis=0)
    flattened = powers.reshape(-1, freq_count)
    smoothed_amplitude = (
        jnp.dot(flattened, banded, precision=lax.Precision.HIGHEST).reshape(powers.shape) / tallies
    )
    amplitude = jnp.sqrt(smoothed_amplitude + EPSILON)
    return spectra / amplitude[..., None, :]


def arrange(field):
    win_count, chan_count, _, freq_count = field.shape
    return field.transpose(3, 1, 0, 2).reshape(freq_count, chan_count, win_count * 2)


def pair_blocks(spectra, offsets, windows):
    nearer = passed_along(spectra, "chan", 1)
    farther = passed_along(spectra, "chan", 2)
    win_count, chan_count, _, freq_count = spectra.shape
    flipped = jnp.stack([spectra[:, :, 1], -spectra[:, :, 0]], axis=2)
    left = jnp.concatenate([arrange(spectra), arrange(flipped)], axis=1)
    right = jnp.concatenate([arrange(spectra), arrange(nearer), arrange(farther)], axis=1)
    joined = jnp.einsum("fik,fjk->fij", left, right, precision=lax.Precision.HIGHEST) / windows
    joined = joined.reshape(freq_count, 2, chan_count, 3, chan_count)
    slots = []
    for position in range(offsets.shape[0]):
        chosen = offsets[position]
        slots.append(
            jnp.where(
                chosen == 0,
                joined[:, :, :, 0],
                jnp.where(chosen == 1, joined[:, :, :, 1], joined[:, :, :, 2]),
            )
        )
    stacked = jnp.stack(slots, axis=0)
    return stacked.transpose(3, 0, 2, 4, 1)


def shards(samples, pair_offsets, spectral_slot_position):
    win_count, sensor_total, segment_span = samples.shape
    freq_count = spectral_slot_position.shape[0]
    time_series = samples.reshape(win_count * sensor_total, segment_span)
    base_cos, base_sin, turn_cos, turn_sin = angle_parts(spectral_slot_position)

    def add_block(step, total):
        piece = lax.dynamic_slice_in_dim(time_series, step * TB, TB, 1)
        row_cos = lax.dynamic_slice_in_dim(turn_cos, step, 1, 0)
        row_sin = lax.dynamic_slice_in_dim(turn_sin, step, 1, 0)
        table = block_table(base_cos, base_sin, row_cos, row_sin)
        return total + jnp.dot(piece, table, preferred_element_type=jnp.float32)

    initial = jnp.zeros((win_count * sensor_total, 2 * freq_count), jnp.float32)
    raw_parts = lax.fori_loop(0, segment_span // TB, add_block, initial)
    spectra = jnp.stack([raw_parts[:, :freq_count], -raw_parts[:, freq_count:]], axis=1)
    spectra = spectra.reshape(win_count, sensor_total, 2, freq_count)
    whitened = whiten(spectra, HALF)
    offsets = pair_offsets[0]
    slabs = lax.all_to_all(whitened, "win", split_axis=3, concat_axis=0, tiled=True)
    return pair_blocks(slabs, offsets, slabs.shape[0])


def solution(mesh):
    in_specs = (P("win", "chan", None), P("chan", None), P())
    out_specs = P("chan", None, None, None, "win")
    return jax.shard_map(shards, mesh=mesh, in_specs=in_specs, out_specs=out_specs, check_vma=False)
```

profile of v0, /device:TPU:28, one launch (start us, length us, event | category | flops | bytes accessed | tf_op | source)
XLA Modules:
  0.0 227.4 jit_solution(14979115997876258393)
XLA Ops:
  0.0 0.2 convert_reduce_fusion
  0.2 0.9 fusion.59
  1.1 138.7 %while.16 = (s32[]{:T(128)}, f32[64,2048]{1,0:T(8,128)S(1)}, bf16[64,6144]{1,0:T(8,128)(2,1)}, f32[6,1024]{1,0:T(8,128)S(1)}, f32[6,1024]{1,0:T(8,128)S(1)}, /*i...) while((s32[]{:T(128)}, f32[64,2048]{1,0:T(8,128)S(1)}, ...), condition=%wide.region_1.2_spmd.clone.clone.clone, body=%wide.region_0.1_spmd.clone.clone.clone.sunk | while | flops 297009152 | bytes 9597093 | solution.py:91
  1.2 20.5 %fusion.73 = (bf16[1024,1024]{1,0:T(8,128)(2,1)S(1)}, bf16[1024,1024]{1,0:T(8,128)(2,1)}) fusion(s32[1024]{0:T(1024)} %get-tuple-element.293, f32[1024]{0:T(1024)S(1)} %bitcast.88, f32[1024]{0:T(1024)S(1)} %bitcast.89), kind=kLoop, calls=%fused_computation.20.clone.1 | loop fusion | flops 19922944 | bytes 4206592 | tf_op jit(solution)/shard_map/convert
  21.7 2.6 %fusion.74 = f32[64,2048]{1,0:T(8,128)S(1)} fusion(bf16[1024,1024]{1,0:T(8,128)(2,1)} %get-tuple-element.266, bf16[1024,1024]{1,0:T(8,128)(2,1)S(1)} %get-tuple-element.267, f32[64,2048]{1,0:T(8,128)S(1)} %get-tuple-element.279, pred[]{:T(512)S(6)} %compare.5, bf16[64,6144]{1,0:T(8,128)(2,1)} %get-tuple-element.290, s32[]{:T(128)S(6)} %select_n.219), kind=kOutput, calls=%fused_computation.25.clone.1 | convolution fusion | flops 277086208 | bytes 5373957 | tf_op jit(solution)/shard_map/while/body/eval_jaxpr/dot_general | solution.py:88
  24.3 20.5 %fusion.73 = (bf16[1024,1024]{1,0:T(8,128)(2,1)S(1)}, bf16[1024,1024]{1,0:T(8,128)(2,1)}) fusion(s32[1024]{0:T(1024)} %get-tuple-element.293, f32[1024]{0:T(1024)S(1)} %bitcast.88, f32[1024]{0:T(1024)S(1)} %bitcast.89), kind=kLoop, calls=%fused_computation.20.clone.1 | loop fusion | flops 19922944 | bytes 4206592 | tf_op jit(solution)/shard_map/convert
  44.8 2.6 %fusion.74 = f32[64,2048]{1,0:T(8,128)S(1)} fusion(bf16[1024,1024]{1,0:T(8,128)(2,1)} %get-tuple-element.266, bf16[1024,1024]{1,0:T(8,128)(2,1)S(1)} %get-tuple-element.267, f32[64,2048]{1,0:T(8,128)S(1)} %get-tuple-element.279, pred[]{:T(512)S(6)} %compare.5, bf16[64,6144]{1,0:T(8,128)(2,1)} %get-tuple-element.290, s32[]{:T(128)S(6)} %select_n.219), kind=kOutput, calls=%fused_computation.25.clone.1 | convolution fusion | flops 277086208 | bytes 5373957 | tf_op jit(solution)/shard_map/while/body/eval_jaxpr/dot_general | solution.py:88
  47.4 20.5 %fusion.73 = (bf16[1024,1024]{1,0:T(8,128)(2,1)S(1)}, bf16[1024,1024]{1,0:T(8,128)(2,1)}) fusion(s32[1024]{0:T(1024)} %get-tuple-element.293, f32[1024]{0:T(1024)S(1)} %bitcast.88, f32[1024]{0:T(1024)S(1)} %bitcast.89), kind=kLoop, calls=%fused_computation.20.clone.1 | loop fusion | flops 19922944 | bytes 4206592 | tf_op jit(solution)/shard_map/convert
  67.9 2.6 %fusion.74 = f32[64,2048]{1,0:T(8,128)S(1)} fusion(bf16[1024,1024]{1,0:T(8,128)(2,1)} %get-tuple-element.266, bf16[1024,1024]{1,0:T(8,128)(2,1)S(1)} %get-tuple-element.267, f32[64,2048]{1,0:T(8,128)S(1)} %get-tuple-element.279, pred[]{:T(512)S(6)} %compare.5, bf16[64,6144]{1,0:T(8,128)(2,1)} %get-tuple-element.290, s32[]{:T(128)S(6)} %select_n.219), kind=kOutput, calls=%fused_computation.25.clone.1 | convolution fusion | flops 277086208 | bytes 5373957 | tf_op jit(solution)/shard_map/while/body/eval_jaxpr/dot_general | solution.py:88
  70.5 20.5 %fusion.73 = (bf16[1024,1024]{1,0:T(8,128)(2,1)S(1)}, bf16[1024,1024]{1,0:T(8,128)(2,1)}) fusion(s32[1024]{0:T(1024)} %get-tuple-element.293, f32[1024]{0:T(1024)S(1)} %bitcast.88, f32[1024]{0:T(1024)S(1)} %bitcast.89), kind=kLoop, calls=%fused_computation.20.clone.1 | loop fusion | flops 19922944 | bytes 4206592 | tf_op jit(solution)/shard_map/convert
  91.0 2.6 %fusion.74 = f32[64,2048]{1,0:T(8,128)S(1)} fusion(bf16[1024,1024]{1,0:T(8,128)(2,1)} %get-tuple-element.266, bf16[1024,1024]{1,0:T(8,128)(2,1)S(1)} %get-tuple-element.267, f32[64,2048]{1,0:T(8,128)S(1)} %get-tuple-element.279, pred[]{:T(512)S(6)} %compare.5, bf16[64,6144]{1,0:T(8,128)(2,1)} %get-tuple-element.290, s32[]{:T(128)S(6)} %select_n.219), kind=kOutput, calls=%fused_computation.25.clone.1 | convolution fusion | flops 277086208 | bytes 5373957 | tf_op jit(solution)/shard_map/while/body/eval_jaxpr/dot_general | solution.py:88
  93.7 20.5 %fusion.73 = (bf16[1024,1024]{1,0:T(8,128)(2,1)S(1)}, bf16[1024,1024]{1,0:T(8,128)(2,1)}) fusion(s32[1024]{0:T(1024)} %get-tuple-element.293, f32[1024]{0:T(1024)S(1)} %bitcast.88, f32[1024]{0:T(1024)S(1)} %bitcast.89), kind=kLoop, calls=%fused_computation.20.clone.1 | loop fusion | flops 19922944 | bytes 4206592 | tf_op jit(solution)/shard_map/convert
  114.2 2.6 %fusion.74 = f32[64,2048]{1,0:T(8,128)S(1)} fusion(bf16[1024,1024]{1,0:T(8,128)(2,1)} %get-tuple-element.266, bf16[1024,1024]{1,0:T(8,128)(2,1)S(1)} %get-tuple-element.267, f32[64,2048]{1,0:T(8,128)S(1)} %get-tuple-element.279, pred[]{:T(512)S(6)} %compare.5, bf16[64,6144]{1,0:T(8,128)(2,1)} %get-tuple-element.290, s32[]{:T(128)S(6)} %select_n.219), kind=kOutput, calls=%fused_computation.25.clone.1 | convolution fusion | flops 277086208 | bytes 5373957 | tf_op jit(solution)/shard_map/while/body/eval_jaxpr/dot_general | solution.py:88
  116.8 20.5 %fusion.73 = (bf16[1024,1024]{1,0:T(8,128)(2,1)S(1)}, bf16[1024,1024]{1,0:T(8,128)(2,1)}) fusion(s32[1024]{0:T(1024)} %get-tuple-element.293, f32[1024]{0:T(1024)S(1)} %bitcast.88, f32[1024]{0:T(1024)S(1)} %bitcast.89), kind=kLoop, calls=%fused_computation.20.clone.1 | loop fusion | flops 19922944 | bytes 4206592 | tf_op jit(solution)/shard_map/convert
  137.3 2.6 %fusion.74 = f32[64,2048]{1,0:T(8,128)S(1)} fusion(bf16[1024,1024]{1,0:T(8,128)(2,1)} %get-tuple-element.266, bf16[1024,1024]{1,0:T(8,128)(2,1)S(1)} %get-tuple-element.267, f32[64,2048]{1,0:T(8,128)S(1)} %get-tuple-element.279, pred[]{:T(512)S(6)} %compare.5, bf16[64,6144]{1,0:T(8,128)(2,1)} %get-tuple-element.290, s32[]{:T(128)S(6)} %select_n.219), kind=kOutput, calls=%fused_computation.25.clone.1 | convolution fusion | flops 277086208 | bytes 5373957 | tf_op jit(solution)/shard_map/while/body/eval_jaxpr/dot_general | solution.py:88
  139.9 0.1 multiply_add_fusion
  140.0 0.9 fusion.52
  140.8 0.1 maximum_divide_fusion
  140.9 1.4 copy.35
  142.2 2.2 reshape.161
  144.5 0.0 copy-start.1
  144.5 11.4 %all_to_all.18 = f32[4,1,32768]{2,1,0:T(1,128)S(1)} all-to-all(f32[4,1,32768]{2,1,0:T(1,128)S(1)} %reshape.161), channel_id=1, replica_groups=mesh['chan'=8,'win'=4] {'win'}, dimensions={0} | all-to-all | bytes 1048576 | tf_op jit(solution)/shard_map/all_to_all | solution.py:96
  155.8 0.5 broadcast.93
  156.4 2.1 reduce
  158.5 1.8 reshape.162
  160.3 0.9 copy.36
  161.2 1.3 collective-permute-start
  162.5 1.5 collective-permute-start.1
  164.0 0.0 copy-done.1
  164.0 0.6 fusion.65
  168.4 2.3 copy.38
  170.6 1.5 copy.37
  172.1 4.4 %collective-permute-done = f32[8,32,2,256]{3,1,2,0:T(8,128)} collective-permute-done((f32[8,32,2,256]{3,1,2,0:T(8,128)S(1)}, f32[8,32,2,256]{3,1,2,0:T(8,128)}, u32[]{:S(2)}, u32[]{:S(2)}) %collective-permute-start) | collective-permute-done | bytes 524320 | tf_op jit(solution)/shard_map/ppermute | solution.py:16
  176.5 3.9 %copy.39 = f32[256,32,8,2]{1,3,2,0:T(2,128)} copy(f32[256,32,8,2]{0,1,3,2:T(8,128)} %bitcast.13) | data formatting | bytes 1048576 | tf_op jit(solution)/shard_map/transpose | solution.py:51
  180.4 7.1 %collective-permute-done.1 = f32[8,32,2,256]{3,1,2,0:T(8,128)S(1)} collective-permute-done((f32[8,32,2,256]{3,1,2,0:T(8,128)S(1)}, f32[8,32,2,256]{3,1,2,0:T(8,128)S(1)}, u32[]{:S(2)}, u32[]{:S(2)}) %collective-permute-start.1) | collective-permute-done | bytes 524320 | tf_op jit(solution)/shard_map/ppermute | solution.py:16
  187.6 2.4 %copy.40 = f32[256,32,8,2]{1,3,2,0:T(2,128)} copy(f32[256,32,8,2]{0,1,3,2:T(8,128)S(1)} %bitcast.87) | data formatting | bytes 1048576 | tf_op jit(solution)/shard_map/transpose | solution.py:51
  190.0 18.9 %broadcast_multiply_fusion = f32[256,64,96]{2,1,0:T(8,128)} fusion(f32[256,32,16]{1,2,0:T(8,128)} %bitcast.76, f32[256,32,16]{1,2,0:T(8,128)S(1)} %bitcast.75, f32[256,32,16]{1,2,0:T(8,128)} %bitcast.78, f32[256,32,16]{1,2,0:T(8,128)} %bitcast.77), kind=kOutput, calls=%fused_computation.32 | convolution fusion | flops 304611328 | bytes 8388608 | tf_op jit(solution)/shard_map/fik,fjk->fij/dot_general | solution.py:61
  208.9 8.5 %copy.41 = f32[256,64,96]{0,2,1:T(8,128)} copy(f32[256,64,96]{2,1,0:T(8,128)} %broadcast_multiply_fusion) | data formatting | bytes 12582912 | tf_op jit(solution)/shard_map/div | solution.py:61
  217.4 0.0 copy-start
  217.4 3.7 %select_bitcast_fusion = f32[1,256,2,32,32]{1,4,3,2,0:T(8,128)S(1)} fusion(f32[256,2,32,3,32]{0,4,3,2,1:T(8,128)} %bitcast.73, pred[]{:T(512)} %bitcast.27, pred[]{:T(512)} %bitcast.25), kind=kLoop, calls=%fused_computation.51 | loop fusion | flops 1048576 | bytes 8388610 | tf_op jit(solution)/shard_map/jit(_where)/select_n | solution.py:67
  221.2 0.9 copy-done
  222.1 0.7 fusion.42
  222.8 1.1 maximum_bitcast_fusion
  223.9 3.5 %copy.48 = f32[32,3,2,32,256]{4,3,2,1,0:T(8,128)} copy(f32[32,3,2,32,256]{4,3,0,2,1:T(8,128)S(1)} %maximum_bitcast_fusion) | data formatting | bytes 12582912 | tf_op jit(solution)/shard_map/transpose | solution.py:74
  (10 shorter events, 0.2 us)
Async XLA Ops:
  144.5 19.5 %copy-start.1 = (s32[1,3]{1,0:T(1,128)S(1)}, s32[1,3]{1,0:T(1,128)}, u32[]{:S(2)}) copy-start(s32[1,3]{1,0:T(1,128)} %param.6) | copy-start | bytes 40
  161.2 15.3 %collective-permute-start = (f32[8,32,2,256]{3,1,2,0:T(8,128)S(1)}, f32[8,32,2,256]{3,1,2,0:T(8,128)}, u32[]{:S(2)}, u32[]{:S(2)}) collective-permute-start(f32[8,32,2,256]{3,1,2,0:T(8,128)S(1)} %bitcast.81), channel_id=1, source_target_pairs={{0,4},{4,8},{8,12},{12,16},{16,20},{20,24},{24,28},{1,5},{5,9},{9,... | collective-permute-start | bytes 1572872 | tf_op jit(solution)/shard_map/ppermute | solution.py:16
  162.5 25.1 %collective-permute-start.1 = (f32[8,32,2,256]{3,1,2,0:T(8,128)S(1)}, f32[8,32,2,256]{3,1,2,0:T(8,128)S(1)}, u32[]{:S(2)}, u32[]{:S(2)}) collective-permute-start(f32[8,32,2,256]{3,1,2,0:T(8,128)S(1)} %bitcast.82), channel_id=1, source_target_pairs={{0,8},{4,12},{8,16},{12,20},{16,24},{20,28},{1,9},{5,13},{9,17},{1... | collective-permute-start | bytes 1572872 | tf_op jit(solution)/shard_map/ppermute | solution.py:16
  217.4 4.7 %copy-start = (f32[256,64,96]{0,2,1:T(8,128)S(1)}, f32[256,64,96]{0,2,1:T(8,128)}, u32[]{:S(2)}) copy-start(f32[256,64,96]{0,2,1:T(8,128)} %copy.41) | copy-start | bytes 18874372
where the time goes:
time: 228 us; the launch traced here: 227 us
  other arithmetic  132 us (58%)
  matrix products  35.3 us (15%)
  local copies, waits for them, and re-layouts  30.5 us (13%)
  waiting for transfers between devices  11.5 us (5%)
  blocking collectives  11.4 us (5%)
  between operations  3.83 us (2%)
  starting transfers between devices  2.76 us (1%)
    another operation x6, other arithmetic  123 us
    dot_general x1, matrix products, pair_blocks(): jnp.einsum('fik,fjk->fij', left, right, precision=lax.Precision.HIGHEST)  18.9 us
    dot_general x6, matrix products, add_block(): return total + jnp.dot(piece, table, preferred_element_type=jnp.float32)  15.5 us
    ppermute x2, waiting for transfers between devices, passed_along(): lax.ppermute(value, axis, [(source, source + steps) for source in range(l...  11.5 us
    all_to_all x1, blocking collectives, shards(): lax.all_to_all(whitened, 'win', split_axis=3, concat_axis=0, tiled=True)  11.4 us
    transpose x4, local copies, waits for them, and re-layouts, arrange(): field.transpose(3, 1, 0, 2).reshape(freq_count, chan_count, win_count * 2)  10.1 us
    div x1, local copies, waits for them, and re-layouts, pair_blocks(): jnp.einsum('fik,fjk->fij', left, right, precision=lax.Precision.HIGHEST)  8.54 us
    unnamed x6, local copies, waits for them, and re-layouts  4.95 us
  transfers between devices with their start and end apart: 2, of which 2 were waited for; matrix products, arithmetic and copies ran while one was open for 4% of the time, Pallas kernels for 0%

commit v1 on v0

--- a/solution.py
+++ b/solution.py
@@ -8,6 +8,28 @@
 HALF = 64
 TB = 1024
 EPSILON = 1e-06
+
+
+def in_blocks(x, dim, size):
+    before, after = (x.shape[:dim], x.shape[dim + 1 :])
+    return jnp.moveaxis(x.reshape(*before, size, -1, *after), dim, 0)
+
+
+def joined_along(blocks, dim):
+    lengths = list(blocks.shape[1:])
+    lengths[dim] *= blocks.shape[0]
+    return jnp.moveaxis(blocks, 0, dim).reshape(lengths)
+
+
+def exchange_in_pairs(array, axis, split_dim, concat_dim):
+    length, index = (lax.axis_size(axis), lax.axis_index(axis))
+    blocks = in_blocks(array, split_dim, length)
+    outs = [blocks[index]]
+    for lap in range(1, length):
+        sent = blocks[index ^ lap]
+        outs.append(lax.ppermute(sent, axis, [(i, i ^ lap) for i in range(length)]))
+    blocks = jnp.stack(outs)[index ^ jnp.arange(length)]
+    return joined_along(blocks, concat_dim)
 
 
 def passed_along(value, axis, steps):
@@ -93,7 +115,7 @@
     spectra = spectra.reshape(win_count, sensor_total, 2, freq_count)
     whitened = whiten(spectra, HALF)
     offsets = pair_offsets[0]
-    slabs = lax.all_to_all(whitened, "win", split_axis=3, concat_axis=0, tiled=True)
+    slabs = exchange_in_pairs(whitened, "win", 3, 0)
     return pair_blocks(slabs, offsets, slabs.shape[0])
 
 

time: 228 us -> 218 us (0.956)
  blocking collectives: 11.4 us -> 0 us
  waiting for transfers between devices: 11.5 us -> 18.4 us
  local copies, waits for them, and re-layouts: 30.5 us -> 24.8 us
    all_to_all x1 -> x0, blocking collectives: 11.4 us -> none  [shards(): lax.all_to_all(whitened, 'win', split_axis=3, concat_axis=0, tiled=True)]
    ppermute x0 -> x3, waiting for transfers between devices: none -> 6.45 us  [exchange_in_pairs(): outs.append(lax.ppermute(sent, axis, [(i, i ^ lap) for i in range(length)]))]
    unnamed x6 -> x4, local copies, waits for them, and re-layouts: 4.95 us -> 0.93 us
    another operation x6 -> x7, other arithmetic: 123 us -> 123 us
  transfers between devices with their start and end apart: 2 -> 5, of which waited for: 2 -> 4; matrix products, arithmetic and copies ran while one was open for 4% -> 4% of each run, Pallas kernels for 0% -> 0%
where the time goes in v1:
time: 218 us
  other arithmetic  130 us (60%)
  matrix products  35.3 us (16%)
  local copies, waits for them, and re-layouts  24.8 us (11%)
  waiting for transfers between devices  18.4 us (8%)
  starting transfers between devices  4.97 us (2%)
  between operations  3.94 us (2%)
    another operation x6, other arithmetic  123 us
    dot_general x1, matrix products, pair_blocks(): jnp.einsum('fik,fjk->fij', left, right, precision=lax.Precision.HIGHEST)  18.9 us
    dot_general x6, matrix products, add_block(): return total + jnp.dot(piece, table, preferred_element_type=jnp.float32)  15.5 us
    ppermute x2, waiting for transfers between devices, passed_along(): lax.ppermute(value, axis, [(source, source + steps) for source in range(l...  12 us
    transpose x4, local copies, waits for them, and re-layouts, arrange(): field.transpose(3, 1, 0, 2).reshape(freq_count, chan_count, win_count * 2)  10.1 us
    div x1, local copies, waits for them, and re-layouts, pair_blocks(): jnp.einsum('fik,fjk->fij', left, right, precision=lax.Precision.HIGHEST)  8.54 us
    ppermute x3, waiting for transfers between devices, exchange_in_pairs(): outs.append(lax.ppermute(sent, axis, [(i, i ^ lap) for i in range(length)]))  6.45 us
    select_n x2, other arithmetic, pair_blocks(): jnp.where(chosen == 0, joined[:, :, :, 0], jnp.where(chosen == 1, joined[...  4.45 us
  transfers between devices with their start and end apart: 5, of which 4 were waited for; matrix products, arithmetic and copies ran while one was open for 4% of the time, Pallas kernels for 0%

profile of v1, /device:TPU:28, one launch (start us, length us, event | category | flops | bytes accessed | tf_op | source)
XLA Modules:
  0.0 217.5 jit_solution(15391389886320443147)
XLA Ops:
  0.0 0.2 convert_reduce_fusion
  0.2 0.9 fusion.59
  1.1 138.7 %while.16 = (s32[]{:T(128)}, f32[64,2048]{1,0:T(8,128)S(1)}, bf16[64,6144]{1,0:T(8,128)(2,1)}, f32[6,1024]{1,0:T(8,128)S(1)}, f32[6,1024]{1,0:T(8,128)S(1)}, /*i...) while((s32[]{:T(128)}, f32[64,2048]{1,0:T(8,128)S(1)}, ...), condition=%wide.region_1.2_spmd.clone.clone.clone, body=%wide.region_0.1_spmd.clone.clone.clone.sunk | while | flops 297009152 | bytes 9597093 | solution.py:113
  1.2 20.5 %fusion.74 = (bf16[1024,1024]{1,0:T(8,128)(2,1)S(1)}, bf16[1024,1024]{1,0:T(8,128)(2,1)}) fusion(s32[1024]{0:T(1024)} %get-tuple-element.297, f32[1024]{0:T(1024)S(1)} %bitcast.95, f32[1024]{0:T(1024)S(1)} %bitcast.96), kind=kLoop, calls=%fused_computation.21.clone.1 | loop fusion | flops 19922944 | bytes 4206592 | tf_op jit(solution)/shard_map/convert
  21.7 2.6 %fusion.75 = f32[64,2048]{1,0:T(8,128)S(1)} fusion(bf16[1024,1024]{1,0:T(8,128)(2,1)} %get-tuple-element.270, bf16[1024,1024]{1,0:T(8,128)(2,1)S(1)} %get-tuple-element.271, f32[64,2048]{1,0:T(8,128)S(1)} %get-tuple-element.283, pred[]{:T(512)S(6)} %compare.5, bf16[64,6144]{1,0:T(8,128)(2,1)} %get-tuple-element.294, s32[]{:T(128)S(6)} %select_n.249), kind=kOutput, calls=%fused_computation.26.clone.1 | convolution fusion | flops 277086208 | bytes 5373957 | tf_op jit(solution)/shard_map/while/body/eval_jaxpr/dot_general | solution.py:110
  24.3 20.5 %fusion.74 = (bf16[1024,1024]{1,0:T(8,128)(2,1)S(1)}, bf16[1024,1024]{1,0:T(8,128)(2,1)}) fusion(s32[1024]{0:T(1024)} %get-tuple-element.297, f32[1024]{0:T(1024)S(1)} %bitcast.95, f32[1024]{0:T(1024)S(1)} %bitcast.96), kind=kLoop, calls=%fused_computation.21.clone.1 | loop fusion | flops 19922944 | bytes 4206592 | tf_op jit(solution)/shard_map/convert
  44.8 2.6 %fusion.75 = f32[64,2048]{1,0:T(8,128)S(1)} fusion(bf16[1024,1024]{1,0:T(8,128)(2,1)} %get-tuple-element.270, bf16[1024,1024]{1,0:T(8,128)(2,1)S(1)} %get-tuple-element.271, f32[64,2048]{1,0:T(8,128)S(1)} %get-tuple-element.283, pred[]{:T(512)S(6)} %compare.5, bf16[64,6144]{1,0:T(8,128)(2,1)} %get-tuple-element.294, s32[]{:T(128)S(6)} %select_n.249), kind=kOutput, calls=%fused_computation.26.clone.1 | convolution fusion | flops 277086208 | bytes 5373957 | tf_op jit(solution)/shard_map/while/body/eval_jaxpr/dot_general | solution.py:110
  47.4 20.5 %fusion.74 = (bf16[1024,1024]{1,0:T(8,128)(2,1)S(1)}, bf16[1024,1024]{1,0:T(8,128)(2,1)}) fusion(s32[1024]{0:T(1024)} %get-tuple-element.297, f32[1024]{0:T(1024)S(1)} %bitcast.95, f32[1024]{0:T(1024)S(1)} %bitcast.96), kind=kLoop, calls=%fused_computation.21.clone.1 | loop fusion | flops 19922944 | bytes 4206592 | tf_op jit(solution)/shard_map/convert
  67.9 2.6 %fusion.75 = f32[64,2048]{1,0:T(8,128)S(1)} fusion(bf16[1024,1024]{1,0:T(8,128)(2,1)} %get-tuple-element.270, bf16[1024,1024]{1,0:T(8,128)(2,1)S(1)} %get-tuple-element.271, f32[64,2048]{1,0:T(8,128)S(1)} %get-tuple-element.283, pred[]{:T(512)S(6)} %compare.5, bf16[64,6144]{1,0:T(8,128)(2,1)} %get-tuple-element.294, s32[]{:T(128)S(6)} %select_n.249), kind=kOutput, calls=%fused_computation.26.clone.1 | convolution fusion | flops 277086208 | bytes 5373957 | tf_op jit(solution)/shard_map/while/body/eval_jaxpr/dot_general | solution.py:110
  70.6 20.5 %fusion.74 = (bf16[1024,1024]{1,0:T(8,128)(2,1)S(1)}, bf16[1024,1024]{1,0:T(8,128)(2,1)}) fusion(s32[1024]{0:T(1024)} %get-tuple-element.297, f32[1024]{0:T(1024)S(1)} %bitcast.95, f32[1024]{0:T(1024)S(1)} %bitcast.96), kind=kLoop, calls=%fused_computation.21.clone.1 | loop fusion | flops 19922944 | bytes 4206592 | tf_op jit(solution)/shard_map/convert
  91.0 2.6 %fusion.75 = f32[64,2048]{1,0:T(8,128)S(1)} fusion(bf16[1024,1024]{1,0:T(8,128)(2,1)} %get-tuple-element.270, bf16[1024,1024]{1,0:T(8,128)(2,1)S(1)} %get-tuple-element.271, f32[64,2048]{1,0:T(8,128)S(1)} %get-tuple-element.283, pred[]{:T(512)S(6)} %compare.5, bf16[64,6144]{1,0:T(8,128)(2,1)} %get-tuple-element.294, s32[]{:T(128)S(6)} %select_n.249), kind=kOutput, calls=%fused_computation.26.clone.1 | convolution fusion | flops 277086208 | bytes 5373957 | tf_op jit(solution)/shard_map/while/body/eval_jaxpr/dot_general | solution.py:110
  93.7 20.5 %fusion.74 = (bf16[1024,1024]{1,0:T(8,128)(2,1)S(1)}, bf16[1024,1024]{1,0:T(8,128)(2,1)}) fusion(s32[1024]{0:T(1024)} %get-tuple-element.297, f32[1024]{0:T(1024)S(1)} %bitcast.95, f32[1024]{0:T(1024)S(1)} %bitcast.96), kind=kLoop, calls=%fused_computation.21.clone.1 | loop fusion | flops 19922944 | bytes 4206592 | tf_op jit(solution)/shard_map/convert
  114.2 2.6 %fusion.75 = f32[64,2048]{1,0:T(8,128)S(1)} fusion(bf16[1024,1024]{1,0:T(8,128)(2,1)} %get-tuple-element.270, bf16[1024,1024]{1,0:T(8,128)(2,1)S(1)} %get-tuple-element.271, f32[64,2048]{1,0:T(8,128)S(1)} %get-tuple-element.283, pred[]{:T(512)S(6)} %compare.5, bf16[64,6144]{1,0:T(8,128)(2,1)} %get-tuple-element.294, s32[]{:T(128)S(6)} %select_n.249), kind=kOutput, calls=%fused_computation.26.clone.1 | convolution fusion | flops 277086208 | bytes 5373957 | tf_op jit(solution)/shard_map/while/body/eval_jaxpr/dot_general | solution.py:110
  116.8 20.5 %fusion.74 = (bf16[1024,1024]{1,0:T(8,128)(2,1)S(1)}, bf16[1024,1024]{1,0:T(8,128)(2,1)}) fusion(s32[1024]{0:T(1024)} %get-tuple-element.297, f32[1024]{0:T(1024)S(1)} %bitcast.95, f32[1024]{0:T(1024)S(1)} %bitcast.96), kind=kLoop, calls=%fused_computation.21.clone.1 | loop fusion | flops 19922944 | bytes 4206592 | tf_op jit(solution)/shard_map/convert
  137.3 2.6 %fusion.75 = f32[64,2048]{1,0:T(8,128)S(1)} fusion(bf16[1024,1024]{1,0:T(8,128)(2,1)} %get-tuple-element.270, bf16[1024,1024]{1,0:T(8,128)(2,1)S(1)} %get-tuple-element.271, f32[64,2048]{1,0:T(8,128)S(1)} %get-tuple-element.283, pred[]{:T(512)S(6)} %compare.5, bf16[64,6144]{1,0:T(8,128)(2,1)} %get-tuple-element.294, s32[]{:T(128)S(6)} %select_n.249), kind=kOutput, calls=%fused_computation.26.clone.1 | convolution fusion | flops 277086208 | bytes 5373957 | tf_op jit(solution)/shard_map/while/body/eval_jaxpr/dot_general | solution.py:110
  139.9 0.1 multiply_add_fusion
  140.0 0.9 fusion.52
  140.8 0.0 copy-start.1
  140.9 0.1 stack.31
  141.0 0.1 copy.25
  141.1 0.1 stack.32
  141.2 0.1 copy.26
  141.3 0.1 maximum_divide_fusion
  141.3 0.1 dynamic-slice_bitcast_fusion.3
  141.4 1.0 collective-permute-start.2
  142.4 0.7 collective-permute-start
  143.1 0.5 collective-permute-start.1
  143.6 3.6 %collective-permute-done.2 = f32[2,32,2,256]{3,1,2,0:T(8,128)S(1)} collective-permute-done((f32[2,32,2,256]{3,1,2,0:T(8,128)S(1)}, f32[2,32,2,256]{3,1,2,0:T(8,128)S(1)}, u32[]{:S(2)}, u32[]{:S(2)}) %collective-permute-start.2) | collective-permute-done | bytes 131104 | tf_op jit(solution)/shard_map/ppermute | solution.py:30
  147.2 0.0 collective-permute-done
  147.2 2.8 %collective-permute-done.1 = f32[2,32,2,256]{3,1,2,0:T(8,128)S(1)} collective-permute-done((f32[2,32,2,256]{3,1,2,0:T(8,128)S(1)}, f32[2,32,2,256]{3,1,2,0:T(8,128)S(1)}, u32[]{:S(2)}, u32[]{:S(2)}) %collective-permute-start.1) | collective-permute-done | bytes 131104 | tf_op jit(solution)/shard_map/ppermute | solution.py:30
  150.1 0.6 gather_fusion
  150.7 1.3 collective-permute-start.3
  152.0 1.5 collective-permute-start.4
  153.5 0.0 copy-done.1
  153.5 0.6 fusion.66
  158.0 2.3 %copy.29 = f32[256,32,8,2]{1,3,2,0:T(2,128)} copy(f32[256,32,8,2]{0,1,3,2:T(8,128)S(1)} %maximum_bitcast_fusion.1) | data formatting | bytes 1048576 | tf_op jit(solution)/shard_map/transpose | solution.py:73
  160.2 1.5 copy.28
  161.8 4.8 %collective-permute-done.3 = f32[8,32,2,256]{3,1,2,0:T(8,128)} collective-permute-done((f32[8,32,2,256]{3,1,2,0:T(8,128)S(1)}, f32[8,32,2,256]{3,1,2,0:T(8,128)}, u32[]{:S(2)}, u32[]{:S(2)}) %collective-permute-start.3) | collective-permute-done | bytes 524320 | tf_op jit(solution)/shard_map/ppermute | solution.py:38
  166.6 3.9 %copy.30 = f32[256,32,8,2]{1,3,2,0:T(2,128)} copy(f32[256,32,8,2]{0,1,3,2:T(8,128)} %bitcast.17) | data formatting | bytes 1048576 | tf_op jit(solution)/shard_map/transpose | solution.py:73
  170.5 7.1 %collective-permute-done.4 = f32[8,32,2,256]{3,1,2,0:T(8,128)S(1)} collective-permute-done((f32[8,32,2,256]{3,1,2,0:T(8,128)S(1)}, f32[8,32,2,256]{3,1,2,0:T(8,128)S(1)}, u32[]{:S(2)}, u32[]{:S(2)}) %collective-permute-start.4) | collective-permute-done | bytes 524320 | tf_op jit(solution)/shard_map/ppermute | solution.py:38
  177.7 2.4 %copy.31 = f32[256,32,8,2]{1,3,2,0:T(2,128)} copy(f32[256,32,8,2]{0,1,3,2:T(8,128)S(1)} %bitcast.94) | data formatting | bytes 1048576 | tf_op jit(solution)/shard_map/transpose | solution.py:73
  180.0 18.9 %broadcast_multiply_fusion = f32[256,64,96]{2,1,0:T(8,128)} fusion(f32[256,32,16]{1,2,0:T(8,128)} %bitcast.86, f32[256,32,16]{1,2,0:T(8,128)S(1)} %bitcast.85, f32[256,32,16]{1,2,0:T(8,128)} %bitcast.88, f32[256,32,16]{1,2,0:T(8,128)} %bitcast.87), kind=kOutput, calls=%fused_computation.33 | convolution fusion | flops 304611328 | bytes 8388608 | tf_op jit(solution)/shard_map/fik,fjk->fij/dot_general | solution.py:83
  199.0 8.5 %copy.32 = f32[256,64,96]{0,2,1:T(8,128)} copy(f32[256,64,96]{2,1,0:T(8,128)} %broadcast_multiply_fusion) | data formatting | bytes 12582912 | tf_op jit(solution)/shard_map/div | solution.py:83
  207.5 3.7 %select_bitcast_fusion = f32[1,256,2,32,32]{1,4,3,2,0:T(8,128)S(1)} fusion(f32[256,2,32,3,32]{0,4,3,2,1:T(8,128)} %bitcast.83, pred[]{:T(512)} %bitcast.31, pred[]{:T(512)} %bitcast.29), kind=kLoop, calls=%fused_computation.52 | loop fusion | flops 1048576 | bytes 8388610 | tf_op jit(solution)/shard_map/jit(_where)/select_n | solution.py:89
  211.2 0.9 copy-done
  212.2 0.7 fusion.42
  212.9 1.1 maximum_bitcast_fusion
  214.0 3.5 %copy.39 = f32[32,3,2,32,256]{4,3,2,1,0:T(8,128)} copy(f32[32,3,2,32,256]{4,3,0,2,1:T(8,128)S(1)} %maximum_bitcast_fusion) | data formatting | bytes 12582912 | tf_op jit(solution)/shard_map/transpose | solution.py:96
  (15 shorter events, 0.2 us)
Async XLA Ops:
  140.8 12.7 %copy-start.1 = (s32[1,3]{1,0:T(1,128)S(1)}, s32[1,3]{1,0:T(1,128)}, u32[]{:S(2)}) copy-start(s32[1,3]{1,0:T(1,128)} %param.6) | copy-start | bytes 40
  141.4 5.8 %collective-permute-start.2 = (f32[2,32,2,256]{3,1,2,0:T(8,128)S(1)}, f32[2,32,2,256]{3,1,2,0:T(8,128)S(1)}, u32[]{:S(2)}, u32[]{:S(2)}) collective-permute-start(f32[2,32,2,256]{3,1,2,0:T(8,128)S(1)} %get-tuple-element.216), channel_id=1, source_target_pairs={{0,3},{1,2},{2,1},{3,0},{4,7},{5,6},{6,5},{7,4},{8,11},{9,10},{10,... | collective-permute-start | bytes 393224 | tf_op jit(solution)/shard_map/ppermute | solution.py:30
  142.4 4.8 %collective-permute-start = (f32[2,32,2,256]{3,1,2,0:T(8,128)S(1)}, f32[2,32,2,256]{3,1,2,0:T(8,128)S(1)}, u32[]{:S(2)}, u32[]{:S(2)}) collective-permute-start(f32[2,32,2,256]{3,1,2,0:T(8,128)S(1)} %get-tuple-element.218), channel_id=1, source_target_pairs={{0,1},{1,0},{2,3},{3,2},{4,5},{5,4},{6,7},{7,6},{8,9},{9,8},{10,11... | collective-permute-start | bytes 393224 | tf_op jit(solution)/shard_map/ppermute | solution.py:30
  143.1 7.0 %collective-permute-start.1 = (f32[2,32,2,256]{3,1,2,0:T(8,128)S(1)}, f32[2,32,2,256]{3,1,2,0:T(8,128)S(1)}, u32[]{:S(2)}, u32[]{:S(2)}) collective-permute-start(f32[2,32,2,256]{3,1,2,0:T(8,128)S(1)} %get-tuple-element.217), channel_id=1, source_target_pairs={{0,2},{1,3},{2,0},{3,1},{4,6},{5,7},{6,4},{7,5},{8,10},{9,11},{10,... | collective-permute-start | bytes 393224 | tf_op jit(solution)/shard_map/ppermute | solution.py:30
  150.7 15.9 %collective-permute-start.3 = (f32[8,32,2,256]{3,1,2,0:T(8,128)S(1)}, f32[8,32,2,256]{3,1,2,0:T(8,128)}, u32[]{:S(2)}, u32[]{:S(2)}) collective-permute-start(f32[8,32,2,256]{3,1,2,0:T(8,128)S(1)} %bitcast.89), channel_id=1, source_target_pairs={{0,4},{4,8},{8,12},{12,16},{16,20},{20,24},{24,28},{1,5},{5,9},{9,... | collective-permute-start | bytes 1572872 | tf_op jit(solution)/shard_map/ppermute | solution.py:38
  152.0 25.7 %collective-permute-start.4 = (f32[8,32,2,256]{3,1,2,0:T(8,128)S(1)}, f32[8,32,2,256]{3,1,2,0:T(8,128)S(1)}, u32[]{:S(2)}, u32[]{:S(2)}) collective-permute-start(f32[8,32,2,256]{3,1,2,0:T(8,128)S(1)} %bitcast.90), channel_id=1, source_target_pairs={{0,8},{4,12},{8,16},{12,20},{16,24},{20,28},{1,9},{5,13},{9,17},{1... | collective-permute-start | bytes 1572872 | tf_op jit(solution)/shard_map/ppermute | solution.py:38
  207.5 4.7 %copy-start = (f32[256,64,96]{0,2,1:T(8,128)S(1)}, f32[256,64,96]{0,2,1:T(8,128)}, u32[]{:S(2)}) copy-start(f32[256,64,96]{0,2,1:T(8,128)} %copy.32) | copy-start | bytes 18874372
